TPU v7x, 32 devices: a whole 2x2x4 slice. The times are simulated.
32 devices in a mesh: groups: 2 (over y), qry: 4 (over x, core), ref: 4 (over z).
Axes of the slice: x: 2, y: 2, z: 4, core: 2. Of those that a mesh axis runs over, the one named last changes fastest.
Arguments:
- query_feats: bfloat16 [1024, 9, 3840], P(('groups', 'qry')), parts along dimension 0, may hold values from -6 to 6
- ref_feats: bfloat16 [256, 4, 9, 3840], P(('groups', 'ref'), 'qry'), parts along dimension 0, may hold values from -6 to 6
- pair_table: int32 [8, 4], P('groups'), parts along dimension 0, may hold values from 0 to 1, as said below
- lengths: int32 [4], P('groups'), parts along dimension 0, may hold values from 1 to 96, 128 in all
- query_len: int32 [2], P('groups'), parts along dimension 0, may hold values from 64 to 128
- conv1_weight: float32 [3, 3, 32], replicated, may hold values from -2 to 2
- conv1_bias: float32 [32], replicated, may hold values from -3 to 3
- conv2_weight: bfloat16 [3, 3, 64, 32], replicated, may hold values from -0.375 to 0.375
- conv2_bias: float32 [64], replicated, may hold values from -3 to 3
- conv3_weight: bfloat16 [3, 3, 128, 64], replicated, may hold values from -0.25 to 0.25
- conv3_bias: float32 [128], replicated, may hold values from -3 to 3
- conv4_weight: bfloat16 [128], replicated, may hold values from -0.5 to 0.5
- conv4_bias: float32 [1], replicated, may hold values from -3 to 3
Outputs:
- score_map: float32 [256, 128], P(('groups', 'qry'), 'ref'), parts along dimension 0
- video_scores: float32 [4], P('groups'), parts along dimension 0
There are 2 independent parts, one for each index of `groups`. A program takes and returns all parts, laid end to end along the dimension named above; an argument that names none is the same for every part. Nothing has to cross between parts.
Inputs may be any that keep to these rules, and one draw needn't show every extreme that they name: `pair_table`: in each row, at most 1 of the 1 tiles in the block of one index of ref are 1, and some such block holds exactly 1 in every draw.
All inputs are finite; a program needn't handle non-finite values.
Results may differ from a plain program's by a relative error of at most 0.01.
Values may be sent and summed in bfloat16 or wider, within the bound.
No kernel may reach another device: no remote copies, remote signals or barrier semaphores. Data moves between devices by JAX's collectives and lax.ppermute only.
A program may use at most 128 MiB of HBM per device.

v0:
```python
import math
import jax
import jax.numpy as jnp
from jax import lax
from jax.sharding import PartitionSpec as P

MOST = 1


def padded_2(block, sides, width):
    for axis, dim in sides:
        count = lax.axis_size(axis)
        forward = [(i, i + 1) for i in range(count - 1)]
        backward = [(target, source) for source, target in forward]
        low = lax.ppermute(
            lax.slice_in_dim(block, block.shape[dim] - width, None, axis=dim), axis, forward
        )
        high = lax.ppermute(lax.slice_in_dim(block, 0, width, axis=dim), axis, backward)
        block = jnp.concatenate([low, block, high], axis=dim)
    return block


def slot_table(mask, most):
    width = mask.shape[-1]
    ranking = jnp.cumsum(mask, axis=-1) - 1
    slot_ids = jnp.arange(most, dtype=jnp.int32)
    chosen = (mask[..., None, :] == 1) & (ranking[..., None, :] == slot_ids[:, None])
    picked = jnp.sum(jnp.where(chosen, jnp.arange(width, dtype=jnp.int32), 0), axis=-1)
    return (chosen, picked)


def frame_sims(query_mat, ref_mat, regions):
    products = lax.dot_general(
        query_mat, ref_mat, (((1,), (1,)), ((), ())), preferred_element_type=jnp.float32
    )
    frames = query_mat.shape[0] // regions
    others = ref_mat.shape[0] // regions
    best = jnp.max(products.reshape(frames, regions, others, regions), axis=3)
    return jnp.sum(best, axis=1) * (1.0 / (regions * math.sqrt(query_mat.shape[1])))


def conv_layer(padded, weights, bias, block_rows, use_pool):
    channels = padded.shape[0]
    height = padded.shape[1] - 2
    width = padded.shape[2] - 2
    block_rows = math.gcd(height, block_rows)
    outputs = weights.shape[0]
    accuracy = lax.Precision.HIGHEST if padded.dtype == jnp.float32 else None

    def one_block(position):
        window = lax.dynamic_slice_in_dim(padded, position * block_rows, block_rows + 2, 1)
        stacked = jnp.concatenate(
            [
                window[:, shift_row : shift_row + block_rows, shift_col : shift_col + width]
                for shift_row in range(3)
                for shift_col in range(3)
            ],
            axis=0,
        )
        result = jnp.dot(
            weights,
            stacked.reshape(9 * channels, block_rows * width),
            preferred_element_type=jnp.float32,
            precision=accuracy,
        )
        result = (result + bias[:, None]).reshape(outputs, block_rows, width)
        result = jnp.maximum(result, 0.0)
        if use_pool:
            result = jnp.max(
                result.reshape(outputs, block_rows // 2, 2, width // 2, 2), axis=(2, 4)
            )
        return result

    blocks = lax.map(one_block, jnp.arange(height // block_rows, dtype=jnp.int32))
    return jnp.transpose(blocks, (1, 0, 2, 3)).reshape(outputs, -1, blocks.shape[-1])


def weight_matrix(weight):
    return jnp.transpose(weight, (2, 0, 1, 3)).reshape(weight.shape[2], -1)


def body(
    query_feats,
    ref_feats,
    pair_table,
    lengths,
    query_len,
    conv1_weight,
    conv1_bias,
    conv2_weight,
    conv2_bias,
    conv3_weight,
    conv3_bias,
    conv4_weight,
    conv4_bias,
):
    qry_index = lax.axis_index("qry")
    ref_index = lax.axis_index("ref")
    frames = query_feats.shape[0]
    regions = query_feats.shape[1]
    channels = query_feats.shape[2]
    tiles_here = pair_table.shape[1] // lax.axis_size("ref")
    tile_rows = ref_feats.shape[0] // tiles_here
    query_mat = query_feats.reshape(frames * regions, channels)
    own_mask = lax.dynamic_slice(pair_table, (qry_index, ref_index * tiles_here), (1, tiles_here))[
        0
    ]
    chosen, picked = slot_table(own_mask, MOST)
    shards = lax.all_gather(ref_feats, "qry", axis=1, tiled=True)
    senders = shards.shape[1]
    sims = frame_sims(query_mat, shards.reshape(tile_rows * senders * regions, channels), regions)
    sims = sims.reshape(1, frames, tile_rows, senders)
    tile_sims = sims.reshape(MOST, frames, frames)
    placed = jnp.einsum(
        "st,sqf->qtf", chosen.astype(jnp.float32), tile_sims, precision=lax.Precision.HIGHEST
    )
    sim_map = placed.reshape(frames, tiles_here * frames)
    padded = padded_2(sim_map, (("qry", 0), ("ref", 1)), 1)
    first_weights = jnp.transpose(conv1_weight, (2, 0, 1)).reshape(conv1_weight.shape[2], 9)
    first = conv_layer(padded[None], first_weights, conv1_bias, 32, True).astype(jnp.bfloat16)
    padded = padded_2(first, (("qry", 1), ("ref", 2)), 1)
    second = conv_layer(padded, weight_matrix(conv2_weight), conv2_bias, 16, True).astype(
        jnp.bfloat16
    )
    padded = padded_2(second, (("qry", 1), ("ref", 2)), 1)
    third = conv_layer(padded, weight_matrix(conv3_weight), conv3_bias, 16, False).astype(
        jnp.bfloat16
    )
    map_rows = third.shape[1]
    map_cols = third.shape[2]
    score_map = (
        jnp.dot(
            conv4_weight[None],
            third.reshape(third.shape[0], -1),
            preferred_element_type=jnp.float32,
        ).reshape(map_rows, map_cols)
        + conv4_bias[0]
    )
    ends = jnp.cumsum(lengths)
    starts = ends - lengths
    column = ref_index * map_cols + jnp.arange(map_cols, dtype=jnp.int32)
    member = (column[:, None] >= starts[None, :]) & (column[:, None] < ends[None, :])
    peaks = jnp.max(jnp.where(member[None], score_map[:, :, None], -jnp.inf), axis=1)
    peaks = lax.pmax(peaks, "ref")
    row_ids = qry_index * map_rows + jnp.arange(map_rows, dtype=jnp.int32)
    partial_value = jnp.sum(jnp.where((row_ids < query_len[0])[:, None], peaks, 0.0), axis=0)
    totals = lax.psum(partial_value, "qry")
    return (score_map, totals / query_len[0].astype(jnp.float32))


def solution(mesh):
    placed = (
        P(("groups", "qry"), None, None),
        P(("groups", "ref"), "qry", None, None),
        P("groups", None),
        P("groups"),
        P("groups"),
        P(),
        P(),
        P(),
        P(),
        P(),
        P(),
        P(),
        P(),
    )
    return jax.shard_map(
        body,
        mesh=mesh,
        in_specs=placed,
        out_specs=(P(("groups", "qry"), "ref"), P("groups")),
        check_vma=False,
    )
```

profile of v0, /device:TPU:0, one launch (start us, length us, event | category | flops | bytes accessed | tf_op | source)
XLA Modules:
  0.0 248.4 jit_solution(3101193552977106752)
XLA Ops:
  7.2 0.7 all-gather.2.cloned.1.call-update
  7.9 1.3 dynamic_slice.23
  10.5 62.7 %all-gather.2.cloned.1.call-done = bf16[32,4,9,3840]{3,0,2,1:T(8,128)(2,1)} async-done(((bf16[32,1,9,3840]{3,0,2,1:T(8,128)(2,1)}), bf16[32,4,9,3840]{3,0,2,1:T(8,128)(2,1)}) %all-gather.2.cloned.1.call-update) | async-done | bytes 8847376 | tf_op jit(solution)/shard_map/all_gather | solution.py:109
  73.2 8.6 %copy.62 = bf16[32,4,9,3840]{3,1,0,2:T(4,128)(2,1)} copy(bf16[32,4,9,3840]{3,0,2,1:T(8,128)(2,1)} %all-gather.2.cloned.1.call-done) | data formatting | bytes 17694720 | tf_op jit(solution)/shard_map/all_gather | solution.py:109
  81.8 12.7 %reshape.195 = bf16[128,9,3840,1]{2,0,1,3:T(8,128)(2,1)} reshape(bf16[32,4,9,3840]{3,1,0,2:T(4,128)(2,1)} %copy.62) | data formatting | bytes 17694720 | tf_op jit(solution)/shard_map/dot_general | solution.py:33
  94.5 18.8 %fusion.7 = f32[128,9,128]{2,0,1:T(8,128)S(1)} fusion(bf16[128,9,3840,1]{2,0,1,3:T(8,128)(2,1)} %reshape.195, bf16[128,9,3840]{2,0,1:T(8,128)(2,1)} %param.19), kind=kOutput, calls=%fused_computation.40 | convolution fusion | flops 10193338368 | bytes 18284544 | tf_op jit(solution)/shard_map/dot_general | solution.py:33
  113.4 2.2 collective-permute-start
  115.6 1.3 collective-permute-start.1
  116.9 1.7 collective-permute-done.1
  118.7 3.4 %collective-permute-start.2 = (f32[130,1]{1,0:T(8,128)S(1)}, f32[130,1]{1,0:T(8,128)S(1)}, u32[]{:S(2)}, u32[]{:S(2)}) collective-permute-start(f32[130,1]{1,0:T(8,128)S(1)} %get-tuple-element.223), channel_id=1, source_target_pairs={{0,1},{1,2},{2,3},{4,5},{5,6},{6,7},{8,9},{9,10},{10,11},{12,13},{... | collective-permute-start | bytes 1568 | tf_op jit(solution)/shard_map/ppermute | solution.py:15
  122.1 1.3 collective-permute-start.3
  124.1 4.3 %collective-permute-done.3 = f32[130,1]{1,0:T(8,128)S(1)} collective-permute-done((f32[130,1]{1,0:T(8,128)S(1)}, f32[130,1]{1,0:T(8,128)S(1)}, u32[]{:S(2)}, u32[]{:S(2)}) %collective-permute-start.3) | collective-permute-done | bytes 552 | tf_op jit(solution)/shard_map/ppermute | solution.py:18
  128.5 23.2 %while.30 = (s32[]{:T(128)}, bf16[4,32,16,64]{3,2,0,1:T(8,128)(2,1)S(1)}, s32[4]{0:T(128)S(1)}, f32[1,130,130]{2,1,0:T(8,128)S(1)}, f32[32,9]{0,1:T(8,128)S(1)},...) while((s32[]{:T(128)}, ...), condition=%wide.region_4.5_spmd, body=%wide.region_2.4_spmd.sunk | while | flops 14647306 | bytes 2885173 | solution.py:74
  128.5 0.6 dynamic_slice.27
  130.5 0.6 fusion.36
  131.6 2.5 %reduce_max.42 = bf16[32,16,64]{0,2,1:T(8,128)(2,1)S(1)} reduce(bf16[32,16,2,64,2]{0,4,3,2,1:T(2,128)(2,1)S(1)} %bitcast.115, bf16[]{:T(256)} %constant.179..sunk), dimensions={2,4}, to_apply=%region_3.3 | reduce | flops 98304 | bytes 327682 | tf_op jit(solution)/shard_map/while/body/eval_jaxpr/reduce_max | solution.py:69
  134.3 0.6 dynamic_slice.27
  136.3 0.6 fusion.36
  137.4 2.5 %reduce_max.42 = bf16[32,16,64]{0,2,1:T(8,128)(2,1)S(1)} reduce(bf16[32,16,2,64,2]{0,4,3,2,1:T(2,128)(2,1)S(1)} %bitcast.115, bf16[]{:T(256)} %constant.179..sunk), dimensions={2,4}, to_apply=%region_3.3 | reduce | flops 98304 | bytes 327682 | tf_op jit(solution)/shard_map/while/body/eval_jaxpr/reduce_max | solution.py:69
  140.1 0.6 dynamic_slice.27
  142.1 0.6 fusion.36
  143.2 2.5 %reduce_max.42 = bf16[32,16,64]{0,2,1:T(8,128)(2,1)S(1)} reduce(bf16[32,16,2,64,2]{0,4,3,2,1:T(2,128)(2,1)S(1)} %bitcast.115, bf16[]{:T(256)} %constant.179..sunk), dimensions={2,4}, to_apply=%region_3.3 | reduce | flops 98304 | bytes 327682 | tf_op jit(solution)/shard_map/while/body/eval_jaxpr/reduce_max | solution.py:69
  145.9 0.6 dynamic_slice.27
  147.9 0.6 fusion.36
  149.0 2.5 %reduce_max.42 = bf16[32,16,64]{0,2,1:T(8,128)(2,1)S(1)} reduce(bf16[32,16,2,64,2]{0,4,3,2,1:T(2,128)(2,1)S(1)} %bitcast.115, bf16[]{:T(256)} %constant.179..sunk), dimensions={2,4}, to_apply=%region_3.3 | reduce | flops 98304 | bytes 327682 | tf_op jit(solution)/shard_map/while/body/eval_jaxpr/reduce_max | solution.py:69
  151.7 2.7 %collective-permute-start.4 = (bf16[32,1,64]{2,1,0:T(2,128)(2,1)S(1)}, bf16[32,1,64]{2,1,0:T(2,128)(2,1)S(1)}, u32[]{:S(2)}, u32[]{:S(2)}) collective-permute-start(bf16[32,1,64]{2,1,0:T(2,128)(2,1)S(1)} %get-tuple-element.217), channel_id=1, source_target_pairs={{0,4},{4,8},{8,12},{1,5},{5,9},{9,13},{2,6},{6,10},{10,14},{3,7},{... | collective-permute-start | bytes 12296 | tf_op jit(solution)/shard_map/ppermute | solution.py:15
  154.5 1.3 collective-permute-start.5
  155.8 2.7 %collective-permute-done.5 = bf16[32,1,64]{2,1,0:T(2,128)(2,1)S(1)} collective-permute-done((bf16[32,1,64]{2,1,0:T(2,128)(2,1)S(1)}, bf16[32,1,64]{2,1,0:T(2,128)(2,1)S(1)}, u32[]{:S(2)}, u32[]{:S(2)}) %collective-permute-start.5) | collective-permute-done | bytes 4128 | tf_op jit(solution)/shard_map/ppermute | solution.py:18
  159.3 3.4 %collective-permute-start.6 = (bf16[32,66,1]{1,0,2:T(8,128)(2,1)S(1)}, bf16[32,66,1]{1,0,2:T(8,128)(2,1)S(1)}, u32[]{:S(2)}, u32[]{:S(2)}) collective-permute-start(bf16[32,66,1]{1,0,2:T(8,128)(2,1)S(1)} %copy.64), channel_id=1, source_target_pairs={{0,1},{1,2},{2,3},{4,5},{5,6},{6,7},{8,9},{9,10},{10,11},{12,13},{... | collective-permute-start | bytes 12680 | tf_op jit(solution)/shard_map/ppermute | solution.py:15
  163.1 1.5 collective-permute-start.7
  164.8 0.9 copy.66
  165.7 2.9 %collective-permute-done.7 = bf16[32,66,1]{1,0,2:T(8,128)(2,1)S(1)} collective-permute-done((bf16[32,66,1]{1,0,2:T(8,128)(2,1)S(1)}, bf16[32,66,1]{1,0,2:T(8,128)(2,1)S(1)}, u32[]{:S(2)}, u32[]{:S(2)}) %collective-permute-start.7) | collective-permute-done | bytes 4256 | tf_op jit(solution)/shard_map/ppermute | solution.py:18
  168.6 0.9 copy.68
  170.1 32.3 %while.31 = (s32[]{:T(128)}, bf16[4,64,8,32]{1,3,2,0:T(8,128)(2,1)}, s32[4]{0:T(128)S(1)}, bf16[32,66,66]{2,0,1:T(8,128)(2,1)S(1)}, bf16[64,288]{1,0:T(8,128)(2,...) while((s32[]{:T(128)}, ...), condition=%wide.region_7.8_spmd, body=%wide.region_5.7_spmd.sunk | while | flops 37994504 | bytes 4822013 | solution.py:74
  170.1 0.6 dynamic_slice.28
  173.1 0.8 copy.113
  174.0 2.4 concatenate.35
  177.0 0.6 reduce_max.43
  177.6 0.6 bitcast_dynamic-update-slice_fusion.2
  181.2 0.8 copy.113
  182.1 2.4 concatenate.35
  185.0 0.6 reduce_max.43
  185.6 0.6 bitcast_dynamic-update-slice_fusion.2
  189.3 0.8 copy.113
  190.1 2.4 concatenate.35
  193.1 0.6 reduce_max.43
  193.7 0.6 bitcast_dynamic-update-slice_fusion.2
  197.4 0.8 copy.113
  198.2 2.4 concatenate.35
  201.2 0.6 reduce_max.43
  201.8 0.6 bitcast_dynamic-update-slice_fusion.2
  202.4 0.7 fusion.14
  203.1 2.9 %collective-permute-start.8 = (bf16[64,1,32]{0,2,1:T(8,128)(2,1)S(1)}, bf16[64,1,32]{0,2,1:T(8,128)(2,1)S(1)}, u32[]{:S(2)}, u32[]{:S(2)}) collective-permute-start(bf16[64,1,32]{0,2,1:T(8,128)(2,1)S(1)} %get-tuple-element.221), channel_id=1, source_target_pairs={{0,4},{4,8},{8,12},{1,5},{5,9},{9,13},{2,6},{6,10},{10,14},{3,7},{... | collective-permute-start | bytes 12296 | tf_op jit(solution)/shard_map/ppermute | solution.py:15
  206.1 1.3 collective-permute-start.9
  208.1 2.0 collective-permute-done.9
  210.1 0.9 pad_maximum_fusion.6
  211.0 3.4 %collective-permute-start.10 = (bf16[64,34,1]{0,2,1:T(2,128)(2,1)S(1)}, bf16[64,34,1]{0,2,1:T(2,128)(2,1)S(1)}, u32[]{:S(2)}, u32[]{:S(2)}) collective-permute-start(bf16[64,34,1]{0,2,1:T(2,128)(2,1)S(1)} %get-tuple-element.219), channel_id=1, source_target_pairs={{0,1},{1,2},{2,3},{4,5},{5,6},{6,7},{8,9},{9,10},{10,11},{12,13},{... | collective-permute-start | bytes 13064 | tf_op jit(solution)/shard_map/ppermute | solution.py:15
  214.4 1.3 collective-permute-start.11
  215.8 1.1 copy.71
  217.5 2.6 %collective-permute-done.11 = bf16[64,34,1]{0,2,1:T(2,128)(2,1)S(1)} collective-permute-done((bf16[64,34,1]{0,2,1:T(2,128)(2,1)S(1)}, bf16[64,34,1]{0,2,1:T(2,128)(2,1)S(1)}, u32[]{:S(2)}, u32[]{:S(2)}) %collective-permute-start.11) | collective-permute-done | bytes 4384 | tf_op jit(solution)/shard_map/ppermute | solution.py:18
  220.1 1.1 pad_maximum_fusion.2
  221.2 4.8 %while.32 = (s32[]{:T(128)}, bf16[2,128,16,32]{1,3,2,0:T(8,128)(2,1)S(1)}, s32[2]{0:T(128)S(1)}, bf16[64,34,34]{0,2,1:T(8,128)(2,1)S(1)}, bf16[128,576]{1,0:T(8,...) while((s32[]{:T(128)}, ...), condition=%wide.region_9.10_spmd, body=%wide.region_8.9_spmd.sunk | while | flops 75694088 | bytes 3490551 | solution.py:74
  226.6 8.5 %pmax.7 = f32[32,2]{0,1:T(2,128)S(1)} all-reduce(f32[32,2]{0,1:T(2,128)S(1)} %select_reduce_fusion), channel_id=1, replica_groups=mesh['groups'=2,'qry'=4,'ref'=4] {'ref'}, use_global_device_ids=true, to_apply=%region_12.13 | all-reduce | flops 64 | bytes 512 | tf_op jit(solution)/shard_map/pmax | solution.py:144
  235.2 5.8 %psum.7 = f32[2]{0:T(128)S(1)} all-reduce(f32[2]{0:T(128)S(1)} %select_reduce_fusion.1), channel_id=1, replica_groups=mesh['groups'=2,'qry'=4,'ref'=4] {'qry'}, use_global_device_ids=true, to_apply=%region_14.15 | all-reduce | flops 2 | bytes 16 | tf_op jit(solution)/shard_map/psum | solution.py:147
  (167 shorter events, 23.9 us)
Async XLA Ops:
  7.2 218.9 %copy-start = (bf16[128]{0:T(256)(128)(2,1)S(1)}, bf16[128]{0:T(256)(128)(2,1)}, u32[]{:S(2)}) copy-start(bf16[128]{0:T(256)(128)(2,1)} %param.30) | copy-start | bytes 772
  7.2 66.0 %all-gather.2.cloned.1.call-start = ((), (), s32[]{:S(2)}) async-start(), calls=%async_computation | async-start | bytes 11059200 | tf_op jit(solution)/shard_map/all_gather | solution.py:109
  94.5 28.9 %copy-start.6 = (f32[3,3,32]{2,1,0:T(4,128)S(1)}, f32[3,3,32]{2,1,0:T(4,128)}, u32[]{:S(2)}) copy-start(f32[3,3,32]{2,1,0:T(4,128)} %param.24) | copy-start | bytes 3460
  94.5 29.0 %copy-start.7 = (s32[2]{0:T(128)S(1)}, s32[2]{0:T(128)}, u32[]{:S(2)}) copy-start(s32[2]{0:T(128)} %param.22) | copy-start | bytes 28
  94.5 34.0 %copy-start.5 = (f32[32]{0:T(128)S(1)}, f32[32]{0:T(128)}, u32[]{:S(2)}) copy-start(f32[32]{0:T(128)} %param.25) | copy-start | bytes 388
  113.4 3.5 %collective-permute-start = (f32[1,128]{1,0:T(1,128)S(1)}, f32[1,128]{1,0:T(1,128)S(1)}, u32[]{:S(2)}, u32[]{:S(2)}) collective-permute-start(f32[1,128]{1,0:T(1,128)S(1)} %get-tuple-element.225), channel_id=1, source_target_pairs={{0,4},{4,8},{8,12},{1,5},{5,9},{9,13},{2,6},{6,10},{10,14},{3,7},{... | collective-permute-start | bytes 1544 | tf_op jit(solution)/shard_map/ppermute | solution.py:15
  115.6 3.1 %collective-permute-start.1 = (f32[1,128]{1,0:T(1,128)S(1)}, f32[1,128]{1,0:T(1,128)S(1)}, u32[]{:S(2)}, u32[]{:S(2)}) collective-permute-start(f32[1,128]{1,0:T(1,128)S(1)} %get-tuple-element.226), channel_id=1, source_target_pairs={{4,0},{8,4},{12,8},{5,1},{9,5},{13,9},{6,2},{10,6},{14,10},{7,3},{... | collective-permute-start | bytes 1544 | tf_op jit(solution)/shard_map/ppermute | solution.py:18
  118.7 5.3 %collective-permute-start.2 = (f32[130,1]{1,0:T(8,128)S(1)}, f32[130,1]{1,0:T(8,128)S(1)}, u32[]{:S(2)}, u32[]{:S(2)}) collective-permute-start(f32[130,1]{1,0:T(8,128)S(1)} %get-tuple-element.223), channel_id=1, source_target_pairs={{0,1},{1,2},{2,3},{4,5},{5,6},{6,7},{8,9},{9,10},{10,11},{12,13},{... | collective-permute-start | bytes 1568 | tf_op jit(solution)/shard_map/ppermute | solution.py:15
  122.1 6.2 %collective-permute-start.3 = (f32[130,1]{1,0:T(8,128)S(1)}, f32[130,1]{1,0:T(8,128)S(1)}, u32[]{:S(2)}, u32[]{:S(2)}) collective-permute-start(f32[130,1]{1,0:T(8,128)S(1)} %get-tuple-element.224), channel_id=1, source_target_pairs={{1,0},{2,1},{3,2},{5,4},{6,5},{7,6},{9,8},{10,9},{11,10},{13,12},{... | collective-permute-start | bytes 1568 | tf_op jit(solution)/shard_map/ppermute | solution.py:18
  128.5 36.1 %copy-start.1 = (bf16[3,3,64,32]{2,3,1,0:T(8,128)(2,1)S(1)}, bf16[3,3,64,32]{2,3,1,0:T(8,128)(2,1)}, u32[]{:S(2)}) copy-start(bf16[3,3,64,32]{2,3,1,0:T(8,128)(2,1)} %param.26) | copy-start | bytes 110596
  151.7 18.4 %copy-start.3 = (f32[64]{0:T(128)S(1)}, f32[64]{0:T(128)}, u32[]{:S(2)}) copy-start(f32[64]{0:T(128)} %param.27) | copy-start | bytes 772
  151.7 4.1 %collective-permute-start.4 = (bf16[32,1,64]{2,1,0:T(2,128)(2,1)S(1)}, bf16[32,1,64]{2,1,0:T(2,128)(2,1)S(1)}, u32[]{:S(2)}, u32[]{:S(2)}) collective-permute-start(bf16[32,1,64]{2,1,0:T(2,128)(2,1)S(1)} %get-tuple-element.217), channel_id=1, source_target_pairs={{0,4},{4,8},{8,12},{1,5},{5,9},{9,13},{2,6},{6,10},{10,14},{3,7},{... | collective-permute-start | bytes 12296 | tf_op jit(solution)/shard_map/ppermute | solution.py:15
  154.5 4.1 %collective-permute-start.5 = (bf16[32,1,64]{2,1,0:T(2,128)(2,1)S(1)}, bf16[32,1,64]{2,1,0:T(2,128)(2,1)S(1)}, u32[]{:S(2)}, u32[]{:S(2)}) collective-permute-start(bf16[32,1,64]{2,1,0:T(2,128)(2,1)S(1)} %get-tuple-element.218), channel_id=1, source_target_pairs={{4,0},{8,4},{12,8},{5,1},{9,5},{13,9},{6,2},{10,6},{14,10},{7,3},{... | collective-permute-start | bytes 12296 | tf_op jit(solution)/shard_map/ppermute | solution.py:18
  159.3 5.4 %collective-permute-start.6 = (bf16[32,66,1]{1,0,2:T(8,128)(2,1)S(1)}, bf16[32,66,1]{1,0,2:T(8,128)(2,1)S(1)}, u32[]{:S(2)}, u32[]{:S(2)}) collective-permute-start(bf16[32,66,1]{1,0,2:T(8,128)(2,1)S(1)} %copy.64), channel_id=1, source_target_pairs={{0,1},{1,2},{2,3},{4,5},{5,6},{6,7},{8,9},{9,10},{10,11},{12,13},{... | collective-permute-start | bytes 12680 | tf_op jit(solution)/shard_map/ppermute | solution.py:15
  163.1 5.5 %collective-permute-start.7 = (bf16[32,66,1]{1,0,2:T(8,128)(2,1)S(1)}, bf16[32,66,1]{1,0,2:T(8,128)(2,1)S(1)}, u32[]{:S(2)}, u32[]{:S(2)}) collective-permute-start(bf16[32,66,1]{1,0,2:T(8,128)(2,1)S(1)} %copy.65), channel_id=1, source_target_pairs={{1,0},{2,1},{3,2},{5,4},{6,5},{7,6},{9,8},{10,9},{11,10},{13,12},{... | collective-permute-start | bytes 12680 | tf_op jit(solution)/shard_map/ppermute | solution.py:18
  170.1 51.1 %copy-start.4 = (f32[128]{0:T(128)S(1)}, f32[128]{0:T(128)}, u32[]{:S(2)}) copy-start(f32[128]{0:T(128)} %param.29) | copy-start | bytes 1540
  203.1 5.0 %collective-permute-start.8 = (bf16[64,1,32]{0,2,1:T(8,128)(2,1)S(1)}, bf16[64,1,32]{0,2,1:T(8,128)(2,1)S(1)}, u32[]{:S(2)}, u32[]{:S(2)}) collective-permute-start(bf16[64,1,32]{0,2,1:T(8,128)(2,1)S(1)} %get-tuple-element.221), channel_id=1, source_target_pairs={{0,4},{4,8},{8,12},{1,5},{5,9},{9,13},{2,6},{6,10},{10,14},{3,7},{... | collective-permute-start | bytes 12296 | tf_op jit(solution)/shard_map/ppermute | solution.py:15
  206.1 4.0 %collective-permute-start.9 = (bf16[64,1,32]{0,2,1:T(8,128)(2,1)S(1)}, bf16[64,1,32]{0,2,1:T(8,128)(2,1)S(1)}, u32[]{:S(2)}, u32[]{:S(2)}) collective-permute-start(bf16[64,1,32]{0,2,1:T(8,128)(2,1)S(1)} %get-tuple-element.222), channel_id=1, source_target_pairs={{4,0},{8,4},{12,8},{5,1},{9,5},{13,9},{6,2},{10,6},{14,10},{7,3},{... | collective-permute-start | bytes 12296 | tf_op jit(solution)/shard_map/ppermute | solution.py:18
  211.0 6.5 %collective-permute-start.10 = (bf16[64,34,1]{0,2,1:T(2,128)(2,1)S(1)}, bf16[64,34,1]{0,2,1:T(2,128)(2,1)S(1)}, u32[]{:S(2)}, u32[]{:S(2)}) collective-permute-start(bf16[64,34,1]{0,2,1:T(2,128)(2,1)S(1)} %get-tuple-element.219), channel_id=1, source_target_pairs={{0,1},{1,2},{2,3},{4,5},{5,6},{6,7},{8,9},{9,10},{10,11},{12,13},{... | collective-permute-start | bytes 13064 | tf_op jit(solution)/shard_map/ppermute | solution.py:15
  214.4 5.6 %collective-permute-start.11 = (bf16[64,34,1]{0,2,1:T(2,128)(2,1)S(1)}, bf16[64,34,1]{0,2,1:T(2,128)(2,1)S(1)}, u32[]{:S(2)}, u32[]{:S(2)}) collective-permute-start(bf16[64,34,1]{0,2,1:T(2,128)(2,1)S(1)} %get-tuple-element.220), channel_id=1, source_target_pairs={{1,0},{2,1},{3,2},{5,4},{6,5},{7,6},{9,8},{10,9},{11,10},{13,12},{... | collective-permute-start | bytes 13064 | tf_op jit(solution)/shard_map/ppermute | solution.py:18
  226.5 15.1 %copy-start.2 = (f32[32,32]{1,0:T(8,128)}, f32[32,32]{1,0:T(8,128)S(1)}, u32[]{:S(2)}) copy-start(f32[32,32]{1,0:T(8,128)S(1)} %broadcast_add_fusion) | copy-start | bytes 12292
Sparse Core Ops, SparseCore 0:
  9.5 63.5 all-gather.1
where the time goes:
time: 250 us; the launch traced here: 248 us
  waiting for transfers between devices  80 us (32%)
  local copies, waits for them, and re-layouts  63.7 us (25%)
  starting transfers between devices  26 us (10%)
  matrix products  23.9 us (10%)
  between operations  17.1 us (7%)
  other arithmetic  16.3 us (7%)
  blocking collectives  14.3 us (6%)
  loops' own time  7.15 us (3%)
    all_gather x1, waiting for transfers between devices, body(): shards = lax.all_gather(ref_feats, 'qry', axis=1, tiled=True)  62.7 us
    dot_general x1, matrix products, frame_sims(): lax.dot_general(query_mat, ref_mat, (((1,), (1,)), ((), ())), preferred_e...  18.8 us
    ppermute x6, starting transfers between devices, padded_2(): lax.ppermute(lax.slice_in_dim(block, block.shape[dim] - width, None, axis...  18 us
    ppermute x6, waiting for transfers between devices, padded_2(): lax.ppermute(lax.slice_in_dim(block, 0, width, axis=dim), axis, backward)  16.2 us
    dot_general x1, local copies, waits for them, and re-layouts, frame_sims(): lax.dot_general(query_mat, ref_mat, (((1,), (1,)), ((), ())), preferred_e...  12.7 us
    reduce_max x8, other arithmetic, one_block(): jnp.max(result.reshape(outputs, block_rows // 2, 2, width // 2, 2), axis=...  12.3 us
    while x76, local copies, waits for them, and re-layouts  11.5 us
    concatenate x10, local copies, waits for them, and re-layouts, one_block(): jnp.concatenate([window[:, shift_row:shift_row + block_rows, shift_col:sh...  11 us
  transfers between devices with their start and end apart: 13, of which 8 were waited for; matrix products, arithmetic and copies ran while one was open for 2% of the time, Pallas kernels for 0%

commit v1 on v0

--- a/solution.py
+++ b/solution.py
@@ -106,7 +106,12 @@
         0
     ]
     chosen, picked = slot_table(own_mask, MOST)
-    shards = lax.all_gather(ref_feats, "qry", axis=1, tiled=True)
+    ring = [ref_feats]
+    for hop in range(3):
+        ring.append(lax.ppermute(ring[-1], "qry", [(dev, (dev + 1) % 4) for dev in range(4)]))
+    shards = jnp.roll(
+        jnp.concatenate(ring[::-1], axis=1), (lax.axis_index("qry") + 1) * ring[0].shape[1], axis=1
+    )
     senders = shards.shape[1]
     sims = frame_sims(query_mat, shards.reshape(tile_rows * senders * regions, channels), regions)
     sims = sims.reshape(1, frames, tile_rows, senders)

time: 250 us -> 394 us (1.58)
  local copies, waits for them, and re-layouts: 63.7 us -> 204 us
  other arithmetic: 16.3 us -> 40.6 us
  between operations: 17.1 us -> 3.69 us
  waiting for transfers between devices: 80 us -> 70.5 us
    reshape x0 -> x3, local copies, waits for them, and re-layouts: none -> 107 us  [the longest x1 76.5 us: frame_sims(): best = jnp.max(products.reshape(frames, regions, others, regions), axis=3)]
    all_gather x1 -> x0, waiting for transfers between devices: 62.7 us -> none  [body(): shards = lax.all_gather(ref_feats, 'qry', axis=1, tiled=True)]
    ppermute x0 -> x3, waiting for transfers between devices: none -> 53.8 us  [body(): lax.ppermute(ring[-1], 'qry', [(dev, (dev + 1) % 4) for dev in range(4)])]
    unnamed x16 -> x30, local copies, waits for them, and re-layouts: 0.04 us -> 29 us
    reduce_max x0 -> x1, other arithmetic: none -> 24.1 us  [frame_sims(): best = jnp.max(products.reshape(frames, regions, others, regions), axis=3)]
    dynamic_slice x0 -> x2, local copies, waits for them, and re-layouts: none -> 17.6 us  [body(): jnp.roll(jnp.concatenate(ring[::-1], axis=1), (lax.axis_index('qry') + 1)...]
    all_gather x1 -> x0, local copies, waits for them, and re-layouts: 8.6 us -> none  [body(): shards = lax.all_gather(ref_feats, 'qry', axis=1, tiled=True)]
    dot_general x1, local copies, waits for them, and re-layouts: 12.7 us -> 6.91 us  [frame_sims(): lax.dot_general(query_mat, ref_mat, (((1,), (1,)), ((), ())), preferred_e...]
  transfers between devices with their start and end apart: 13 -> 15, of which waited for: 8 -> 9; matrix products, arithmetic and copies ran while one was open for 2% -> 8% of each run, Pallas kernels for 0% -> 0%
where the time goes in v1:
time: 394 us; the launch traced here: 392 us
  local copies, waits for them, and re-layouts  204 us (52%)
  waiting for transfers between devices  70.5 us (18%)
  other arithmetic  40.6 us (10%)
  starting transfers between devices  28.6 us (7%)
  matrix products  22.7 us (6%)
  blocking collectives  14.3 us (4%)
  loops' own time  7.29 us (2%)
    reshape x1, local copies, waits for them, and re-layouts, frame_sims(): best = jnp.max(products.reshape(frames, regions, others, regions), axis=3)  76.5 us
    ppermute x3, waiting for transfers between devices, body(): lax.ppermute(ring[-1], 'qry', [(dev, (dev + 1) % 4) for dev in range(4)])  53.8 us
    unnamed x30, local copies, waits for them, and re-layouts  29 us
    reduce_max x1, other arithmetic, frame_sims(): best = jnp.max(products.reshape(frames, regions, others, regions), axis=3)  24.1 us
    ppermute x6, starting transfers between devices, padded_2(): lax.ppermute(lax.slice_in_dim(block, block.shape[dim] - width, None, axis...  20.1 us
    dot_general x1, matrix products, frame_sims(): lax.dot_general(query_mat, ref_mat, (((1,), (1,)), ((), ())), preferred_e...  17.7 us
    dynamic_slice x2, local copies, waits for them, and re-layouts, body(): jnp.roll(jnp.concatenate(ring[::-1], axis=1), (lax.axis_index('qry') + 1)...  17.6 us
    ppermute x6, waiting for transfers between devices, padded_2(): lax.ppermute(lax.slice_in_dim(block, 0, width, axis=dim), axis, backward)  16.4 us
  transfers between devices with their start and end apart: 15, of which 9 were waited for; matrix products, arithmetic and copies ran while one was open for 8% of the time, Pallas kernels for 0%

profile of v1, /device:TPU:0, one launch (start us, length us, event | category | flops | bytes accessed | tf_op | source)
XLA Modules:
  0.0 392.0 jit_solution(6632788764710456163)
XLA Ops:
  1.2 27.1 %collective-permute-done = bf16[32,1,9,3840]{3,0,2,1:T(8,128)(2,1)S(1)} collective-permute-done((bf16[32,1,9,3840]{3,0,2,1:T(8,128)(2,1)}, bf16[32,1,9,3840]{3,0,2,1:T(8,128)(2,1)S(1)}, u32[]{:S(2)}, u32[]{:S(2)}) %collective-permute-start) | collective-permute-done | bytes 2211872 | tf_op jit(solution)/shard_map/ppermute | solution.py:111
  28.3 1.3 copy-done.2
  29.6 26.8 %collective-permute-done.1 = bf16[32,1,9,3840]{3,0,2,1:T(8,128)(2,1)} collective-permute-done((bf16[32,1,9,3840]{3,0,2,1:T(8,128)(2,1)S(1)}, bf16[32,1,9,3840]{3,0,2,1:T(8,128)(2,1)}, u32[]{:S(2)}, u32[]{:S(2)}) %collective-permute-start.1) | collective-permute-done | bytes 2211872 | tf_op jit(solution)/shard_map/ppermute | solution.py:111
  56.4 10.2 %copy.70 = bf16[128,9,3840]{2,1,0:T(8,128)(2,1)} copy(bf16[128,9,3840]{2,0,1:T(8,128)(2,1)} %param.19) | data formatting | bytes 17694720 | tf_op args[0]
  66.6 15.1 %reshape.192 = bf16[1152,3840]{1,0:T(8,128)(2,1)} reshape(bf16[128,9,3840]{2,1,0:T(8,128)(2,1)} %copy.70) | data formatting | bytes 17694720 | tf_op jit(solution)/shard_map/reshape | solution.py:104
  81.7 1.4 dynamic_slice.28
  84.4 3.3 constant_dynamic-update-slice_fusion.18
  87.7 3.1 constant_dynamic-update-slice_fusion.17
  90.8 1.6 constant_dynamic-update-slice_fusion.16
  92.4 1.6 constant_dynamic-update-slice_fusion.15
  94.0 3.2 constant_dynamic-update-slice_fusion.14
  97.2 3.2 constant_dynamic-update-slice_fusion.13
  100.4 1.5 constant_dynamic-update-slice_fusion.12
  101.9 1.5 constant_dynamic-update-slice_fusion.11
  103.3 7.5 %constant_dynamic-slice_fusion.18 = bf16[32,4,9,3840]{3,0,2,1:T(8,128)(2,1)} fusion(bf16[32,8,9,3840]{3,0,2,1:T(8,128)(2,1)} %constant_dynamic-update-slice_fusion.11, s32[]{:T(128)S(6)} %select_n.37), kind=kLoop, calls=%fused_computation.65 | loop fusion | bytes 17694724 | tf_op jit(solution)/shard_map/jit(_roll_dynamic)/dynamic_slice | solution.py:112
  110.8 10.2 %copy.69 = bf16[32,4,9,3840]{3,2,1,0:T(8,128)(2,1)} copy(bf16[32,4,9,3840]{3,0,2,1:T(8,128)(2,1)} %constant_dynamic-slice_fusion.18) | data formatting | bytes 17694720 | tf_op jit(solution)/shard_map/jit(_roll_dynamic)/dynamic_slice | solution.py:112
  121.0 15.1 %reshape.191 = bf16[1152,3840]{1,0:T(8,128)(2,1)} reshape(bf16[32,4,9,3840]{3,2,1,0:T(8,128)(2,1)} %copy.69) | data formatting | bytes 17694720 | tf_op jit(solution)/shard_map/reshape | solution.py:116
  136.1 17.7 %convolution_bitcast_fusion = f32[1152,1152]{0,1:T(8,128)} fusion(bf16[1152,3840]{1,0:T(8,128)(2,1)} %reshape.191, bf16[1152,3840]{1,0:T(8,128)(2,1)} %reshape.192), kind=kOutput, calls=%fused_computation.38 | convolution fusion | flops 10192158720 | bytes 23003136 | tf_op jit(solution)/shard_map/dot_general | solution.py:33
  153.8 6.9 %copy.71 = f32[1152,1152]{1,0:T(8,128)} copy(f32[1152,1152]{0,1:T(8,128)} %convolution_bitcast_fusion) | data formatting | bytes 10616832 | tf_op jit(solution)/shard_map/dot_general | solution.py:33
  160.7 76.5 %reshape.193 = f32[128,9,128,9]{3,2,1,0:T(8,128)} reshape(f32[1152,1152]{1,0:T(8,128)} %copy.71) | data formatting | bytes 10616832 | tf_op jit(solution)/shard_map/reshape | solution.py:38
  237.2 24.1 %reduce_max.36 = f32[128,9,128]{2,1,0:T(8,128)S(1)} reduce(f32[128,9,128,9]{3,2,1,0:T(8,128)} %reshape.193, f32[]{:T(128)} %constant.107.clone.1), dimensions={3}, to_apply=%region_0.0 | reduce | flops 1179648 | bytes 5898244 | tf_op jit(solution)/shard_map/reduce_max | solution.py:38
  261.6 4.3 %collective-permute-start.3 = (f32[1,128]{1,0:T(1,128)S(1)}, f32[1,128]{1,0:T(1,128)S(1)}, u32[]{:S(2)}, u32[]{:S(2)}) collective-permute-start(f32[1,128]{1,0:T(1,128)S(1)} %get-tuple-element.225), channel_id=1, source_target_pairs={{0,4},{4,8},{8,12},{1,5},{5,9},{9,13},{2,6},{6,10},{10,14},{3,7},{... | collective-permute-start | bytes 1544 | tf_op jit(solution)/shard_map/ppermute | solution.py:15
  265.9 1.3 collective-permute-start.4
  267.2 1.7 collective-permute-done.4
  269.1 3.5 collective-permute-start.5
  272.5 1.5 collective-permute-start.6
  274.5 4.4 %collective-permute-done.6 = f32[130,1]{1,0:T(8,128)S(1)} collective-permute-done((f32[130,1]{1,0:T(8,128)S(1)}, f32[130,1]{1,0:T(8,128)S(1)}, u32[]{:S(2)}, u32[]{:S(2)}) %collective-permute-start.6) | collective-permute-done | bytes 552 | tf_op jit(solution)/shard_map/ppermute | solution.py:18
  279.0 23.2 %while.30 = (s32[]{:T(128)}, bf16[4,32,16,64]{3,2,0,1:T(8,128)(2,1)S(1)}, s32[4]{0:T(128)S(1)}, f32[1,130,130]{2,1,0:T(8,128)S(1)}, f32[32,9]{0,1:T(8,128)S(1)},...) while((s32[]{:T(128)}, ...), condition=%wide.region_4.5_spmd, body=%wide.region_2.4_spmd.sunk | while | flops 14647306 | bytes 2885173 | solution.py:74
  282.1 2.5 reduce_max.41
  287.9 2.5 reduce_max.41
  293.7 2.5 reduce_max.41
  299.5 2.5 reduce_max.41
  302.2 2.4 collective-permute-start.7
  304.6 1.3 collective-permute-start.8
  305.9 2.6 collective-permute-done.8
  309.4 3.5 collective-permute-start.9
  313.2 1.3 collective-permute-start.10
  314.7 0.9 copy.76
  315.7 3.0 collective-permute-done.10
  318.7 0.9 copy.78
  320.2 32.4 %while.31 = (s32[]{:T(128)}, bf16[4,64,8,32]{1,3,2,0:T(8,128)(2,1)}, s32[4]{0:T(128)S(1)}, bf16[32,66,66]{2,0,1:T(8,128)(2,1)S(1)}, bf16[64,288]{1,0:T(8,128)(2,...) while((s32[]{:T(128)}, ...), condition=%wide.region_7.8_spmd, body=%wide.region_5.7_spmd.sunk | while | flops 37994504 | bytes 4822013 | solution.py:74
  323.3 0.9 copy.123
  324.1 2.4 concatenate.42
  327.7 0.6 bitcast_dynamic-update-slice_fusion.2
  331.3 0.9 copy.123
  332.2 2.4 concatenate.42
  339.4 0.9 copy.123
  340.3 2.4 concatenate.42
  343.9 0.6 bitcast_dynamic-update-slice_fusion.2
  347.5 0.9 copy.123
  348.4 2.4 concatenate.42
  352.6 0.7 fusion.9
  353.3 2.9 collective-permute-start.11
  356.3 1.3 collective-permute-start.12
  358.3 2.0 collective-permute-done.12
  360.3 0.9 pad_maximum_fusion.6
  361.2 3.5 collective-permute-start.13
  364.7 1.3 collective-permute-start.14
  366.0 1.1 copy.81
  367.8 2.6 collective-permute-done.14
  370.3 1.1 pad_maximum_fusion.2
  371.5 5.0 %while.32 = (s32[]{:T(128)}, bf16[2,128,16,32]{1,3,2,0:T(8,128)(2,1)S(1)}, s32[2]{0:T(128)S(1)}, bf16[64,34,34]{0,2,1:T(8,128)(2,1)S(1)}, bf16[128,576]{1,0:T(8,...) while((s32[]{:T(128)}, ...), condition=%wide.region_9.10_spmd, body=%wide.region_8.9_spmd.sunk | while | flops 75694088 | bytes 3490551 | solution.py:74
  377.1 8.5 %pmax.7 = f32[32,2]{0,1:T(2,128)S(1)} all-reduce(f32[32,2]{0,1:T(2,128)S(1)} %select_reduce_fusion), channel_id=1, replica_groups=mesh['groups'=2,'qry'=4,'ref'=4] {'ref'}, use_global_device_ids=true, to_apply=%region_12.13 | all-reduce | flops 64 | bytes 512 | tf_op jit(solution)/shard_map/pmax | solution.py:149
  385.7 5.8 %psum.7 = f32[2]{0:T(128)S(1)} all-reduce(f32[2]{0:T(128)S(1)} %select_reduce_fusion.1), channel_id=1, replica_groups=mesh['groups'=2,'qry'=4,'ref'=4] {'qry'}, use_global_device_ids=true, to_apply=%region_14.15 | all-reduce | flops 2 | bytes 16 | tf_op jit(solution)/shard_map/psum | solution.py:152
  (190 shorter events, 33.6 us)
Async XLA Ops:
  0.6 375.9 %copy-start = (bf16[128]{0:T(256)(128)(2,1)S(1)}, bf16[128]{0:T(256)(128)(2,1)}, u32[]{:S(2)}) copy-start(bf16[128]{0:T(256)(128)(2,1)} %param.30) | copy-start | bytes 772
  0.6 27.6 %collective-permute-start = (bf16[32,1,9,3840]{3,0,2,1:T(8,128)(2,1)}, bf16[32,1,9,3840]{3,0,2,1:T(8,128)(2,1)S(1)}, u32[]{:S(2)}, u32[]{:S(2)}) collective-permute-start(bf16[32,1,9,3840]{3,0,2,1:T(8,128)(2,1)} %param.20), channel_id=1, source_target_pairs={{0,4},{4,8},{8,12},{12,0},{1,5},{5,9},{9,13},{13,1},{2,6},{6,10},{... | collective-permute-start | bytes 6635528 | tf_op jit(solution)/shard_map/ppermute | solution.py:111
  28.3 1.3 copy-start.2
  29.6 26.8 %collective-permute-start.1 = (bf16[32,1,9,3840]{3,0,2,1:T(8,128)(2,1)S(1)}, bf16[32,1,9,3840]{3,0,2,1:T(8,128)(2,1)}, u32[]{:S(2)}, u32[]{:S(2)}) collective-permute-start(bf16[32,1,9,3840]{3,0,2,1:T(8,128)(2,1)S(1)} %collective-permute-done), channel_id=1, source_target_pairs={{0,4},{4,8},{8,12},{12,0},{1,5},{5,9},{9,13},{13,1},{2,6},{6,10},{... | collective-permute-start | bytes 6635528 | tf_op jit(solution)/shard_map/ppermute | solution.py:111
  56.4 28.0 %collective-permute-start.2 = (bf16[32,1,9,3840]{3,0,2,1:T(8,128)(2,1)}, bf16[32,1,9,3840]{3,0,2,1:T(8,128)(2,1)}, u32[]{:S(2)}, u32[]{:S(2)}) collective-permute-start(bf16[32,1,9,3840]{3,0,2,1:T(8,128)(2,1)} %collective-permute-done.1), channel_id=1, source_target_pairs={{0,4},{4,8},{8,12},{12,0},{1,5},{5,9},{9,13},{13,1},{2,6},{6,10},{... | collective-permute-start | bytes 6635528 | tf_op jit(solution)/shard_map/ppermute | solution.py:111
  81.7 10.7 %copy-start.1 = (bf16[32,1,9,3840]{3,0,2,1:T(8,128)(2,1)S(1)}, bf16[32,1,9,3840]{3,0,2,1:T(8,128)(2,1)}, u32[]{:S(2)}) copy-start(bf16[32,1,9,3840]{3,0,2,1:T(8,128)(2,1)} %param.20) | copy-start | bytes 6635524
  84.4 6.4 %copy-start.3 = (bf16[32,1,9,3840]{3,0,2,1:T(8,128)(2,1)S(1)}, bf16[32,1,9,3840]{3,0,2,1:T(8,128)(2,1)}, u32[]{:S(2)}) copy-start(bf16[32,1,9,3840]{3,0,2,1:T(8,128)(2,1)} %copy-done.2) | copy-start | bytes 6635524
  237.2 36.8 %copy-start.9 = (f32[3,3,32]{2,1,0:T(4,128)S(1)}, f32[3,3,32]{2,1,0:T(4,128)}, u32[]{:S(2)}) copy-start(f32[3,3,32]{2,1,0:T(4,128)} %param.24) | copy-start | bytes 3460
  237.2 36.8 %copy-start.10 = (s32[2]{0:T(128)S(1)}, s32[2]{0:T(128)}, u32[]{:S(2)}) copy-start(s32[2]{0:T(128)} %param.22) | copy-start | bytes 28
  237.2 41.8 %copy-start.8 = (f32[32]{0:T(128)S(1)}, f32[32]{0:T(128)}, u32[]{:S(2)}) copy-start(f32[32]{0:T(128)} %param.25) | copy-start | bytes 388
  261.6 5.6 %collective-permute-start.3 = (f32[1,128]{1,0:T(1,128)S(1)}, f32[1,128]{1,0:T(1,128)S(1)}, u32[]{:S(2)}, u32[]{:S(2)}) collective-permute-start(f32[1,128]{1,0:T(1,128)S(1)} %get-tuple-element.225), channel_id=1, source_target_pairs={{0,4},{4,8},{8,12},{1,5},{5,9},{9,13},{2,6},{6,10},{10,14},{3,7},{... | collective-permute-start | bytes 1544 | tf_op jit(solution)/shard_map/ppermute | solution.py:15
  265.9 3.1 collective-permute-start.4
  269.1 5.4 %collective-permute-start.5 = (f32[130,1]{1,0:T(8,128)S(1)}, f32[130,1]{1,0:T(8,128)S(1)}, u32[]{:S(2)}, u32[]{:S(2)}) collective-permute-start(f32[130,1]{1,0:T(8,128)S(1)} %get-tuple-element.223), channel_id=1, source_target_pairs={{0,1},{1,2},{2,3},{4,5},{5,6},{6,7},{8,9},{9,10},{10,11},{12,13},{... | collective-permute-start | bytes 1568 | tf_op jit(solution)/shard_map/ppermute | solution.py:15
  272.5 6.3 %collective-permute-start.6 = (f32[130,1]{1,0:T(8,128)S(1)}, f32[130,1]{1,0:T(8,128)S(1)}, u32[]{:S(2)}, u32[]{:S(2)}) collective-permute-start(f32[130,1]{1,0:T(8,128)S(1)} %get-tuple-element.224), channel_id=1, source_target_pairs={{1,0},{2,1},{3,2},{5,4},{6,5},{7,6},{9,8},{10,9},{11,10},{13,12},{... | collective-permute-start | bytes 1568 | tf_op jit(solution)/shard_map/ppermute | solution.py:18
  279.0 35.5 %copy-start.4 = (bf16[3,3,64,32]{2,3,1,0:T(8,128)(2,1)S(1)}, bf16[3,3,64,32]{2,3,1,0:T(8,128)(2,1)}, u32[]{:S(2)}) copy-start(bf16[3,3,64,32]{2,3,1,0:T(8,128)(2,1)} %param.26) | copy-start | bytes 110596
  302.2 18.0 %copy-start.6 = (f32[64]{0:T(128)S(1)}, f32[64]{0:T(128)}, u32[]{:S(2)}) copy-start(f32[64]{0:T(128)} %param.27) | copy-start | bytes 772
  302.2 3.7 collective-permute-start.7
  304.6 4.0 %collective-permute-start.8 = (bf16[32,1,64]{2,1,0:T(2,128)(2,1)S(1)}, bf16[32,1,64]{2,1,0:T(2,128)(2,1)S(1)}, u32[]{:S(2)}, u32[]{:S(2)}) collective-permute-start(bf16[32,1,64]{2,1,0:T(2,128)(2,1)S(1)} %get-tuple-element.218), channel_id=1, source_target_pairs={{4,0},{8,4},{12,8},{5,1},{9,5},{13,9},{6,2},{10,6},{14,10},{7,3},{... | collective-permute-start | bytes 12296 | tf_op jit(solution)/shard_map/ppermute | solution.py:18
  309.4 5.3 %collective-permute-start.9 = (bf16[32,66,1]{1,0,2:T(8,128)(2,1)S(1)}, bf16[32,66,1]{1,0,2:T(8,128)(2,1)S(1)}, u32[]{:S(2)}, u32[]{:S(2)}) collective-permute-start(bf16[32,66,1]{1,0,2:T(8,128)(2,1)S(1)} %copy.74), channel_id=1, source_target_pairs={{0,1},{1,2},{2,3},{4,5},{5,6},{6,7},{8,9},{9,10},{10,11},{12,13},{... | collective-permute-start | bytes 12680 | tf_op jit(solution)/shard_map/ppermute | solution.py:15
  313.2 5.5 %collective-permute-start.10 = (bf16[32,66,1]{1,0,2:T(8,128)(2,1)S(1)}, bf16[32,66,1]{1,0,2:T(8,128)(2,1)S(1)}, u32[]{:S(2)}, u32[]{:S(2)}) collective-permute-start(bf16[32,66,1]{1,0,2:T(8,128)(2,1)S(1)} %copy.75), channel_id=1, source_target_pairs={{1,0},{2,1},{3,2},{5,4},{6,5},{7,6},{9,8},{10,9},{11,10},{13,12},{... | collective-permute-start | bytes 12680 | tf_op jit(solution)/shard_map/ppermute | solution.py:18
  320.2 51.2 %copy-start.7 = (f32[128]{0:T(128)S(1)}, f32[128]{0:T(128)}, u32[]{:S(2)}) copy-start(f32[128]{0:T(128)} %param.29) | copy-start | bytes 1540
  353.3 5.0 %collective-permute-start.11 = (bf16[64,1,32]{0,2,1:T(8,128)(2,1)S(1)}, bf16[64,1,32]{0,2,1:T(8,128)(2,1)S(1)}, u32[]{:S(2)}, u32[]{:S(2)}) collective-permute-start(bf16[64,1,32]{0,2,1:T(8,128)(2,1)S(1)} %get-tuple-element.221), channel_id=1, source_target_pairs={{0,4},{4,8},{8,12},{1,5},{5,9},{9,13},{2,6},{6,10},{10,14},{3,7},{... | collective-permute-start | bytes 12296 | tf_op jit(solution)/shard_map/ppermute | solution.py:15
  356.3 4.0 %collective-permute-start.12 = (bf16[64,1,32]{0,2,1:T(8,128)(2,1)S(1)}, bf16[64,1,32]{0,2,1:T(8,128)(2,1)S(1)}, u32[]{:S(2)}, u32[]{:S(2)}) collective-permute-start(bf16[64,1,32]{0,2,1:T(8,128)(2,1)S(1)} %get-tuple-element.222), channel_id=1, source_target_pairs={{4,0},{8,4},{12,8},{5,1},{9,5},{13,9},{6,2},{10,6},{14,10},{7,3},{... | collective-permute-start | bytes 12296 | tf_op jit(solution)/shard_map/ppermute | solution.py:18
  361.2 6.6 %collective-permute-start.13 = (bf16[64,34,1]{0,2,1:T(2,128)(2,1)S(1)}, bf16[64,34,1]{0,2,1:T(2,128)(2,1)S(1)}, u32[]{:S(2)}, u32[]{:S(2)}) collective-permute-start(bf16[64,34,1]{0,2,1:T(2,128)(2,1)S(1)} %get-tuple-element.219), channel_id=1, source_target_pairs={{0,1},{1,2},{2,3},{4,5},{5,6},{6,7},{8,9},{9,10},{10,11},{12,13},{... | collective-permute-start | bytes 13064 | tf_op jit(solution)/shard_map/ppermute | solution.py:15
  364.7 5.6 %collective-permute-start.14 = (bf16[64,34,1]{0,2,1:T(2,128)(2,1)S(1)}, bf16[64,34,1]{0,2,1:T(2,128)(2,1)S(1)}, u32[]{:S(2)}, u32[]{:S(2)}) collective-permute-start(bf16[64,34,1]{0,2,1:T(2,128)(2,1)S(1)} %get-tuple-element.220), channel_id=1, source_target_pairs={{1,0},{2,1},{3,2},{5,4},{6,5},{7,6},{9,8},{10,9},{11,10},{13,12},{... | collective-permute-start | bytes 13064 | tf_op jit(solution)/shard_map/ppermute | solution.py:18
  377.0 15.1 %copy-start.5 = (f32[32,32]{1,0:T(8,128)}, f32[32,32]{1,0:T(8,128)S(1)}, u32[]{:S(2)}) copy-start(f32[32,32]{1,0:T(8,128)S(1)} %broadcast_add_fusion) | copy-start | bytes 12292
